TPU v7x, 512 devices: a whole 4x4x16 slice. The times are simulated.
512 devices in a mesh: req: 32 (over z, core), mlp: 16 (over y, x).
Axes of the slice: x: 4, y: 4, z: 16, core: 2. Of those that a mesh axis runs over, the one named last changes fastest.
Arguments:
- hidden_input: bfloat16 [12288, 4096], P('req', 'mlp'), may hold values from -6 to 6
- input_norm_gain: bfloat16 [4096], replicated, may hold values from 0.099609375 to 1.8984375
- query_norm_gain: bfloat16 [128], replicated, may hold values from 0.099609375 to 1.8984375
- key_norm_gain: bfloat16 [128], replicated, may hold values from 0.099609375 to 1.8984375
- query_weight: bfloat16 [4096, 4096], P('req', 'mlp'), may hold values from -0.09375 to 0.09375
- key_value_weight: bfloat16 [4096, 2, 1024], P('req'), may hold values from -0.09375 to 0.09375
- output_weight: bfloat16 [4096, 16, 256], P('mlp', None, 'req'), may hold values from -0.09375 to 0.09375
- adapter_down_qkv: bfloat16 [64, 48, 4096], P('req', None, 'mlp'), may hold values from -0.09375 to 0.09375
- adapter_down_output: bfloat16 [64, 16, 4096], P('req', None, 'mlp'), may hold values from -0.09375 to 0.09375
- adapter_up_query: bfloat16 [64, 16, 4096], P('req', None, 'mlp'), may hold values from -1.5 to 1.5
- adapter_up_key_value: bfloat16 [64, 16, 2, 1024], P('req'), may hold values from -1.5 to 1.5
- adapter_up_output: bfloat16 [64, 16, 4096], P('req', None, 'mlp'), may hold values from -1.5 to 1.5
- pool: bfloat16 [16384, 2, 1024], P('req'), may hold values from -6 to 6
- lengths: int32 [32, 4], P('req'), may hold values from 1 to 192, 384 in all within a row
- cached_prefix_pages: int32 [32, 4], P('req'), may hold values from 0 to 8
- prefix_page_table: int32 [32, 4, 8], P('req'), may hold values from 0 to 7, each once within a row
- adapter_of_request: int32 [32, 4, 1], P('req'), may hold values from 0 to 63
- adapter_storage: int32 [64], replicated, may hold values from 0 to 63, each once
Outputs:
- attention_update: bfloat16 [12288, 4096], P('req', 'mlp')
- new_cache: bfloat16 [12288, 2, 1024], P('req', None, 'mlp')
Inputs may be any that keep to these rules, and one draw needn't show every extreme that they name: The lengths of one index of req sum to 384, and the longest of them is 192. `prefix_page_table`: each row lists every page of its pool once. `adapter_of_request`: every adapter is used by some request. `adapter_storage`: each slot holds one adapter.
All inputs are finite; a program needn't handle non-finite values.
Results may differ from a plain program's by a relative error of at most 0.035.
Values may be sent and summed in bfloat16 or wider, within the bound.
A program may use at most 64 MiB of HBM per device.

v0:
```python
import math
import jax
import jax.numpy as jnp
from jax import lax
from jax.sharding import PartitionSpec as P

QUERY_HEADS = 32
KEY_VALUE_HEADS = 8
HEAD_SIZE = 128
ADAPTER_RANK = 16
PAGE = 64
epsilon = 1e-06
rope_base = 1000000.0


def root_mean_scale(values, gain_vec):
    mean_sq = jnp.mean(values * values, axis=-1, keepdims=True)
    return values * lax.rsqrt(mean_sq + epsilon) * gain_vec.astype(jnp.float32)


def rotary_embed(values, token_positions):
    half_width = values.shape[-1] // 2
    inverse_freq = jnp.exp(
        jnp.arange(half_width, dtype=jnp.float32) * (-2.0 / values.shape[-1]) * math.log(rope_base)
    )
    angles = token_positions.astype(jnp.float32)[:, None] * inverse_freq[None, :]
    cosine = jnp.cos(angles)[:, None, :]
    sine_part = jnp.sin(angles)[:, None, :]
    front = values[..., :half_width]
    back = values[..., half_width:]
    return jnp.concatenate(
        [front * cosine - back * sine_part, back * cosine + front * sine_part], axis=-1
    )


def row_tables(lengths_row, prefix_row, page_rows, row_count):
    ends_at = jnp.cumsum(lengths_row)
    starts_at = ends_at - lengths_row
    row_ids = jnp.arange(row_count, dtype=jnp.int32)
    owners = jnp.sum((row_ids[:, None] >= ends_at[None, :]).astype(jnp.int32), axis=1)
    group_members = owners[:, None] == jnp.arange(lengths_row.shape[0], dtype=jnp.int32)[None, :]
    offsets = PAGE * prefix_row[None, :] + row_ids[:, None] - starts_at[None, :]
    token_positions = jnp.sum(jnp.where(group_members, offsets, 0), axis=1)
    page_ids = jnp.arange(page_rows.shape[1], dtype=jnp.int32)
    listed = (page_rows[:, :, None] == page_ids[None, None, :]) & (
        page_ids[None, :, None] < prefix_row[:, None, None]
    )
    page_used = jnp.sum(listed.astype(jnp.float32), axis=1)
    return (owners, group_members, token_positions, page_used)


def apply_adapter(lowrank_inner, group_members, chosen_up):
    masked = lowrank_inner[:, None, :] * group_members.astype(lowrank_inner.dtype)[:, :, None]
    return jnp.einsum("gjr,jrc->gc", masked, chosen_up, preferred_element_type=jnp.float32)


def select_rows(terms, group_members):
    return jnp.sum(terms * group_members.astype(jnp.float32)[:, :, None], axis=1)


def shards(
    hidden_input,
    input_norm_gain,
    query_norm_gain,
    key_norm_gain,
    query_weight,
    key_value_weight,
    output_weight,
    adapter_down_qkv,
    adapter_down_output,
    adapter_up_query,
    adapter_up_key_value,
    adapter_up_output,
    pool,
    lengths,
    cached_prefix_pages,
    prefix_page_table,
    adapter_of_request,
    adapter_storage,
):
    feature_group_count = lax.axis_size("mlp")
    feature_group_index = lax.axis_index("mlp")
    whole = lax.all_gather(hidden_input, "mlp", axis=1, tiled=True)
    row_count, full_width = whole.shape
    normalized_input = root_mean_scale(whole.astype(jnp.float32), input_norm_gain).astype(
        jnp.bfloat16
    )
    owners, group_members, token_positions, page_used = row_tables(
        lengths[0], cached_prefix_pages[0], prefix_page_table[0], row_count
    )
    q_width = query_weight.shape[1]
    query_head_rows = q_width // HEAD_SIZE
    key_value_local = max(1, KEY_VALUE_HEADS // feature_group_count)
    key_value_width = key_value_local * HEAD_SIZE
    key_value_begin = (
        feature_group_index * query_head_rows // (QUERY_HEADS // KEY_VALUE_HEADS) * HEAD_SIZE
    )
    own_wkv = lax.dynamic_slice_in_dim(key_value_weight, key_value_begin, key_value_width, 2)
    request_key_value_up = lax.dynamic_slice_in_dim(
        adapter_up_key_value, key_value_begin, key_value_width, 3
    )
    gathered = (
        lax.all_gather(adapter_down_qkv, "req", axis=0, tiled=True),
        lax.all_gather(adapter_down_output, "req", axis=0, tiled=True),
        lax.all_gather(adapter_up_query, "req", axis=0, tiled=True),
        lax.all_gather(request_key_value_up, "req", axis=0, tiled=True),
        lax.all_gather(adapter_up_output, "req", axis=0, tiled=True),
    )
    slot_indices = jnp.take(adapter_storage, adapter_of_request[0, :, 0], axis=0)
    chosen_down = jnp.take(gathered[0], slot_indices, axis=0)
    output_down = jnp.take(gathered[1], slot_indices, axis=0)
    query_up_part = jnp.take(gathered[2], slot_indices, axis=0)
    key_value_up = jnp.take(gathered[3], slot_indices, axis=0)
    output_up = jnp.take(gathered[4], slot_indices, axis=0)
    feature_cols = full_width // feature_group_count
    own_normed = lax.dynamic_slice_in_dim(
        normalized_input, feature_group_index * feature_cols, feature_cols, 1
    )
    low_terms = jnp.einsum(
        "gd,jkd->gjk", own_normed, chosen_down, preferred_element_type=jnp.float32
    )
    lowrank_inner = lax.psum(select_rows(low_terms, group_members).astype(jnp.bfloat16), "mlp")
    q_part = lax.all_gather(query_weight, "req", axis=0, tiled=True)
    kv_part = lax.all_gather(own_wkv, "req", axis=0, tiled=True)
    query_width_total = jnp.dot(normalized_input, q_part, preferred_element_type=jnp.float32)
    kv_total = jnp.dot(
        normalized_input,
        kv_part.reshape(kv_part.shape[0], 2 * key_value_width),
        preferred_element_type=jnp.float32,
    )
    query_width_total, kv_total = (query_width_total, kv_total)
    query_plain = (
        query_width_total
        + apply_adapter(lowrank_inner[:, 0:ADAPTER_RANK], group_members, query_up_part)
    ).astype(jnp.bfloat16)
    key_lowrank_part = apply_adapter(
        lowrank_inner[:, ADAPTER_RANK : 2 * ADAPTER_RANK], group_members, key_value_up[:, :, 0]
    )
    value_lowrank_part = apply_adapter(
        lowrank_inner[:, 2 * ADAPTER_RANK : 3 * ADAPTER_RANK], group_members, key_value_up[:, :, 1]
    )
    key_value_plain = (
        kv_total.reshape(row_count, 2, key_value_width)
        + jnp.stack([key_lowrank_part, value_lowrank_part], axis=1)
    ).astype(jnp.bfloat16)
    cached = lax.dynamic_slice_in_dim(pool, key_value_begin, key_value_width, 2)
    pool_token_rows = cached.shape[0]
    query_rotated = rotary_embed(
        root_mean_scale(
            query_plain.astype(jnp.float32).reshape(row_count, query_head_rows, HEAD_SIZE),
            query_norm_gain,
        ),
        token_positions,
    ).astype(jnp.bfloat16)
    key_rotated = rotary_embed(
        root_mean_scale(
            key_value_plain[:, 0]
            .astype(jnp.float32)
            .reshape(row_count, key_value_local, HEAD_SIZE),
            key_norm_gain,
        ),
        token_positions,
    ).astype(jnp.bfloat16)
    cache_columns = KEY_VALUE_HEADS * HEAD_SIZE // feature_group_count
    own_offset = feature_group_index * cache_columns - key_value_begin
    local_cache = jnp.stack(
        [key_rotated.reshape(row_count, key_value_width), key_value_plain[:, 1]], axis=1
    )
    new_cache = lax.dynamic_slice_in_dim(local_cache, own_offset, cache_columns, 2)
    key_matrix = jnp.concatenate(
        [cached[:, 0].reshape(pool_token_rows, key_value_local, HEAD_SIZE), key_rotated], axis=0
    )
    value_matrix = jnp.concatenate(
        [
            cached[:, 1].reshape(pool_token_rows, key_value_local, HEAD_SIZE),
            key_value_plain[:, 1].reshape(row_count, key_value_local, HEAD_SIZE),
        ],
        axis=0,
    )
    pool_ok = jnp.dot(group_members.astype(jnp.float32), page_used, precision=lax.Precision.HIGHEST)
    pool_ok = jnp.repeat(pool_ok, PAGE, axis=1) > 0.5
    row_ids = jnp.arange(row_count, dtype=jnp.int32)
    causal = (owners[:, None] == owners[None, :]) & (row_ids[None, :] <= row_ids[:, None])
    allowed = jnp.concatenate([pool_ok, causal], axis=1)
    query_rows = query_rotated.reshape(
        row_count, key_value_local, query_head_rows // key_value_local, HEAD_SIZE
    )
    scores = jnp.einsum(
        "gkhd,skd->khgs", query_rows, key_matrix, preferred_element_type=jnp.float32
    ) / math.sqrt(HEAD_SIZE)
    exp_scores = jnp.where(allowed[None, None], jnp.exp(scores), 0.0)
    softmax = (exp_scores / jnp.sum(exp_scores, axis=-1, keepdims=True)).astype(jnp.bfloat16)
    attended = jnp.einsum(
        "khgs,skd->gkhd", softmax, value_matrix, preferred_element_type=jnp.float32
    )
    attended = attended.astype(jnp.bfloat16).reshape(row_count, q_width)
    out_terms = jnp.einsum("gc,jrc->gjr", attended, output_down, preferred_element_type=jnp.float32)
    lowrank_result = lax.psum(select_rows(out_terms, group_members), "mlp").astype(jnp.bfloat16)
    partial_value = jnp.einsum(
        "gc,cnk->gnk",
        attended,
        lax.all_gather(output_weight, "req", axis=2, tiled=True),
        preferred_element_type=jnp.float32,
    )
    summed_output = lax.psum_scatter(
        partial_value.reshape(row_count, full_width).astype(jnp.bfloat16),
        "mlp",
        scatter_dimension=1,
        tiled=True,
    ).astype(jnp.float32)
    attention_update = (
        summed_output + apply_adapter(lowrank_result, group_members, output_up)
    ).astype(jnp.bfloat16)
    return (attention_update, new_cache)


def solution(mesh):
    return jax.shard_map(
        shards,
        mesh=mesh,
        in_specs=(
            P("req", "mlp"),
            P(),
            P(),
            P(),
            P("req", "mlp"),
            P("req", None, None),
            P("mlp", None, "req"),
            P("req", None, "mlp"),
            P("req", None, "mlp"),
            P("req", None, "mlp"),
            P("req", None, None, None),
            P("req", None, "mlp"),
            P("req", None, None),
            P("req", None),
            P("req", None),
            P("req", None, None),
            P("req", None, None),
            P(),
        ),
        out_specs=(P("req", "mlp"), P("req", None, "mlp")),
        check_vma=False,
    )
```

profile of v0, /device:TPU:32, one launch (start us, length us, event | category | flops | bytes accessed | tf_op | source)
XLA Modules:
  0.0 518.9 jit_solution(2938642543624137017)
XLA Ops:
  7.3 0.7 all-gather.10.cloned.1.call-update
  8.0 0.2 copy-done
  8.2 0.7 constant_dynamic-slice_fusion.2
  9.0 0.7 all-gather.6.cloned.1.call-update
  9.7 0.5 all-gather.12.cloned.1.call-update
  10.3 0.5 all-gather.14.cloned.1.call-update
  10.9 0.7 fusion.90
  11.6 1.3 gather_fusion
  12.9 0.7 fusion.80
  13.5 0.7 compare_and_fusion
  14.2 0.8 reduce-window.4
  15.0 0.7 fusion.81
  15.8 0.6 fusion.76
  16.4 0.1 fusion.28
  16.5 0.7 constant_dynamic-slice_fusion.1
  17.3 36.1 %all_gather.30 = bf16[64,16,2,128]{3,1,2,0:T(8,128)(2,1)S(1)} all-gather(bf16[2,16,2,128]{3,1,2,0:T(8,128)(2,1)S(1)} %copy.66), channel_id=1, replica_groups=mesh['req'=32,'mlp'=16] {'req'}, dimensions={0}, use_global_device_ids=true | all-gather | bytes 540672 | tf_op jit(solution)/shard_map/all_gather | solution.py:106
  53.3 0.7 convert_element_type.100
  54.0 1.2 convert_element_type.109
  55.2 0.7 multiply_bitcast_fusion
  55.9 0.1 select_reduce_fusion
  56.0 1.6 constant_dynamic-slice_fusion
  57.6 30.2 %all_gather.32 = bf16[64,16,256]{2,1,0:T(8,128)(2,1)S(1)} all-gather(bf16[2,16,256]{2,1,0:T(8,128)(2,1)S(1)} %copy-done.6), channel_id=1, replica_groups=mesh['req'=32,'mlp'=16] {'req'}, dimensions={0}, use_global_device_ids=true | all-gather | bytes 540672 | tf_op jit(solution)/shard_map/all_gather | solution.py:105
  87.8 0.5 convert_element_type.112
  88.4 0.1 convert_reduce_fusion
  88.5 0.2 convolution_compare_fusion
  88.7 0.7 copy.65
  89.4 0.6 gather_fusion.2
  90.0 0.7 copy_select_fusion
  90.7 1.2 gather_fusion.3
  91.8 0.8 multiply_cosine_fusion
  92.8 2.6 gather_fusion.1
  95.4 61.2 %all-gather.8.cloned.1.call-done = bf16[4096,2,128]{2,1,0:T(2,128)(2,1)} async-done(((bf16[128,2,128]{2,1,0:T(2,128)(2,1)}), bf16[4096,2,128]{2,1,0:T(2,128)(2,1)}) %all-gather.8.cloned.1.call-update) | async-done | bytes 2097168 | tf_op jit(solution)/shard_map/all_gather | solution.py:124
  156.6 4.7 copy.61
  161.3 63.1 %all-gather.6.cloned.1.call-done = bf16[384,4096]{1,0:T(8,128)(2,1)} async-done(((bf16[384,256]{1,0:T(8,128)(2,1)}), bf16[384,4096]{1,0:T(8,128)(2,1)}) %all-gather.6.cloned.1.call-update) | async-done | bytes 3145744 | tf_op jit(solution)/shard_map/all_gather | solution.py:83
  224.4 2.7 fusion
  227.2 0.1 copy-done.1
  227.3 1.1 fusion.2
  228.4 1.6 copy-done.2
  230.0 0.9 fusion.26
  230.9 72.8 %psum.14 = bf16[384,48]{0,1:T(8,128)(2,1)S(1)} all-reduce(bf16[384,48]{0,1:T(8,128)(2,1)} %fusion.26), channel_id=1, replica_groups=mesh['req'=32,'mlp'=16] {'mlp'}, use_global_device_ids=true, to_apply=%region_4.5 | all-reduce | flops 18432 | bytes 73728 | tf_op jit(solution)/shard_map/psum | solution.py:122
  303.7 0.9 convolution_bitcast_fusion.2
  304.7 0.9 convolution_bitcast_fusion.3
  305.6 3.2 fusion.17
  309.0 0.4 fusion.46
  309.5 0.1 copy.53
  309.6 3.8 fusion.92
  313.5 0.4 multiply_reduce_fusion
  313.8 0.1 copy.54
  314.0 0.1 copy.52
  314.1 0.2 multiply_multiply_fusion
  314.3 0.2 subtract_convert_fusion
  314.5 0.9 fusion.5
  315.5 0.9 fusion.23
  316.4 53.5 %all-gather.14.cloned.1.call-done = bf16[256,16,256]{0,2,1:T(8,128)(2,1)} async-done(((bf16[256,16,8]{0,2,1:T(8,128)(2,1)}), bf16[256,16,256]{0,2,1:T(8,128)(2,1)}) %all-gather.14.cloned.1.call-update) | async-done | bytes 2097168 | tf_op jit(solution)/shard_map/all_gather | solution.py:202
  369.9 4.3 convolution_convert_fusion
  374.2 0.7 copy-done.7
  374.9 28.9 %all_gather.34 = bf16[64,16,256]{2,1,0:T(8,128)(2,1)S(1)} all-gather(bf16[2,16,256]{2,1,0:T(8,128)(2,1)S(1)} %copy-done.7), channel_id=1, replica_groups=mesh['req'=32,'mlp'=16] {'req'}, dimensions={0}, use_global_device_ids=true | all-gather | bytes 540672 | tf_op jit(solution)/shard_map/all_gather | solution.py:104
  403.8 0.5 gather_fusion.4
  404.3 30.1 %all_gather.35 = bf16[64,16,256]{2,1,0:T(8,128)(2,1)S(1)} all-gather(bf16[2,16,256]{2,1,0:T(8,128)(2,1)S(1)} %copy-done.8), channel_id=1, replica_groups=mesh['req'=32,'mlp'=16] {'req'}, dimensions={0}, use_global_device_ids=true | all-gather | bytes 540672 | tf_op jit(solution)/shard_map/all_gather | solution.py:107
  434.4 0.5 gather_fusion.5
  435.0 0.2 fusion.27
  435.2 74.3 %psum.15 = bf16[384,16]{0,1:T(8,128)(2,1)S(1)} all-reduce(f32[384,16]{0,1:T(8,128)S(1)} %fusion.27), channel_id=1, replica_groups=mesh['req'=32,'mlp'=16] {'mlp'}, use_global_device_ids=true, to_apply=%region_12.14 | all-reduce | flops 6144 | bytes 36864 | tf_op jit(solution)/shard_map/psum | solution.py:198
  509.5 0.7 fusion.50
  510.2 1.9 fusion.16
  (62 shorter events, 0.9 us)
Async XLA Ops:
  7.2 1.1 copy-start
  7.2 81.2 %copy-start.17 = (s32[1,4]{1,0:T(1,128)S(1)}, s32[1,4]{1,0:T(1,128)}, u32[]{:S(2)}) copy-start(s32[1,4]{1,0:T(1,128)} %param.34) | copy-start | bytes 52
  7.2 50.4 %copy-start.6 = (bf16[2,16,256]{2,1,0:T(8,128)(2,1)S(1)}, bf16[2,16,256]{2,1,0:T(8,128)(2,1)}, u32[]{:S(2)}) copy-start(bf16[2,16,256]{2,1,0:T(8,128)(2,1)} %param.29) | copy-start | bytes 49156
  7.2 80.6 %copy-start.16 = (bf16[128]{0:T(256)(128)(2,1)S(1)}, bf16[128]{0:T(256)(128)(2,1)}, u32[]{:S(2)}) copy-start(bf16[128]{0:T(256)(128)(2,1)} %param.22) | copy-start | bytes 772
  7.2 81.2 %copy-start.13 = (s32[1,4,8]{2,1,0:T(4,128)S(1)}, s32[1,4,8]{2,1,0:T(4,128)}, u32[]{:S(2)}) copy-start(s32[1,4,8]{2,1,0:T(4,128)} %param.35) | copy-start | bytes 388
  7.2 85.5 %all-gather.10.cloned.1.call-start = ((), (), s32[]{:S(2)}) async-start(), calls=%async_computation.3 | async-start | bytes 1622016 | tf_op jit(solution)/shard_map/all_gather | solution.py:103
  8.0 148.6 %all-gather.8.cloned.1.call-start = ((), (), s32[]{:S(2)}) async-start(), calls=%async_computation.2 | async-start | bytes 2162688 | tf_op jit(solution)/shard_map/all_gather | solution.py:124
  8.9 215.5 %all-gather.6.cloned.1.call-start = ((), (), s32[]{:S(2)}) async-start(), calls=%async_computation.1 | async-start | bytes 3342336 | tf_op jit(solution)/shard_map/all_gather | solution.py:83
  9.7 299.9 %all-gather.12.cloned.1.call-start = ((), (), s32[]{:S(2)}) async-start(), calls=%async_computation.4 | async-start | bytes 2162688 | tf_op jit(solution)/shard_map/all_gather | solution.py:123
  10.3 359.6 %all-gather.14.cloned.1.call-start = ((), (), s32[]{:S(2)}) async-start(), calls=%async_computation.5 | async-start | bytes 2162688 | tf_op jit(solution)/shard_map/all_gather | solution.py:202
  10.8 499.4 %reduce-scatter.2.cloned.1.call-start = ((), (), s32[]{:S(2)}) async-start(), calls=%async_computation.6 | async-start | bytes 3342336 | tf_op jit(solution)/shard_map/reduce_scatter | solution.py:205
  14.2 147.1 %copy-start.11 = (f32[64]{0:T(128)}, f32[64]{0:T(128)S(1)}, u32[]{:S(2)}) copy-start(f32[64]{0:T(128)S(1)} %multiply_exponential_fusion) | copy-start | bytes 772
  224.4 2.8 copy-start.1
  227.3 2.8 copy-start.5
  227.3 2.8 copy-start.9
  228.4 1.7 copy-start.2
  305.6 3.3 copy-start.14
  305.6 3.4 copy-start.12
  309.6 3.9 copy-start.4
  309.6 4.5 copy-start.15
  314.3 1.2 copy-start.3
  374.1 0.7 copy-start.7
  374.1 30.2 %copy-start.8 = (bf16[2,16,256]{2,1,0:T(8,128)(2,1)S(1)}, bf16[2,16,256]{2,1,0:T(8,128)(2,1)}, u32[]{:S(2)}) copy-start(bf16[2,16,256]{2,1,0:T(8,128)(2,1)} %param.31) | copy-start | bytes 49156
  374.1 60.9 %copy-start.10 = (f32[384,4]{0,1:T(4,128)S(1)}, f32[384,4]{0,1:T(4,128)}, u32[]{:S(2)}) copy-start(f32[384,4]{0,1:T(4,128)} %get-tuple-element.17) | copy-start | bytes 18436
Sparse Core Ops, SparseCore 0:
  10.2 75.3 all-gather.9
  87.7 68.8 all-gather.7
  159.6 64.8 all-gather.5
  226.4 71.1 all-gather.11
  299.5 70.3 all-gather.13
  374.3 87.2 reduce-scatter.1
where the time goes:
time: 520 us; the launch traced here: 519 us
  blocking collectives  272 us (52%)
  waiting for transfers between devices  180 us (35%)
  matrix products  18.5 us (4%)
  local copies, waits for them, and re-layouts  18.3 us (4%)
  other arithmetic  14.7 us (3%)
  between operations  14.6 us (3%)
    psum x1, blocking collectives, shards(): lax.psum(select_rows(out_terms, group_members), 'mlp').astype(jnp.bfloat16)  74.3 us
    psum x1, blocking collectives, shards(): lax.psum(select_rows(low_terms, group_members).astype(jnp.bfloat16), 'mlp')  72.8 us
    all_gather x1, waiting for transfers between devices, shards(): whole = lax.all_gather(hidden_input, 'mlp', axis=1, tiled=True)  63.1 us
    all_gather x1, waiting for transfers between devices, shards(): kv_part = lax.all_gather(own_wkv, 'req', axis=0, tiled=True)  61.2 us
    all_gather x1, waiting for transfers between devices, shards(): lax.all_gather(output_weight, 'req', axis=2, tiled=True)  53.5 us
    all_gather x1, blocking collectives, shards(): lax.all_gather(request_key_value_up, 'req', axis=0, tiled=True)  36.1 us
    all_gather x1, blocking collectives, shards(): lax.all_gather(adapter_up_query, 'req', axis=0, tiled=True)  30.2 us
    all_gather x1, blocking collectives, shards(): lax.all_gather(adapter_up_output, 'req', axis=0, tiled=True)  30.1 us
  transfers between devices with their start and end apart: 6, of which 3 were waited for; matrix products, arithmetic and copies ran while one was open for 8% of the time, Pallas kernels for 0%

commit v1 on v0

--- a/solution.py
+++ b/solution.py
@@ -195,7 +195,10 @@
     )
     attended = attended.astype(jnp.bfloat16).reshape(row_count, q_width)
     out_terms = jnp.einsum("gc,jrc->gjr", attended, output_down, preferred_element_type=jnp.float32)
-    lowrank_result = lax.psum(select_rows(out_terms, group_members), "mlp").astype(jnp.bfloat16)
+    assign_frame_over_axis = lambda vector, mesh_dim: lax.all_gather(vector, mesh_dim).sum(axis=0)
+    lowrank_result = assign_frame_over_axis(select_rows(out_terms, group_members), "mlp").astype(
+        jnp.bfloat16
+    )
     partial_value = jnp.einsum(
         "gc,cnk->gnk",
         attended,

time: 520 us -> 471 us (0.906)
  blocking collectives: 272 us -> 223 us
    psum x1 -> x0, blocking collectives: 74.3 us -> none  [shards(): lax.psum(select_rows(out_terms, group_members), 'mlp').astype(jnp.bfloat16)]
    all_gather x0 -> x1, blocking collectives: none -> 24.6 us  [shards(): lax.all_gather(vector, mesh_dim).sum(axis=0)]
  transfers between devices with their start and end apart: 6 -> 6, of which waited for: 3 -> 4; matrix products, arithmetic and copies ran while one was open for 8% -> 9% of each run, Pallas kernels for 0% -> 0%
where the time goes in v1:
time: 471 us; the launch traced here: 470 us
  blocking collectives  223 us (47%)
  waiting for transfers between devices  181 us (38%)
  matrix products  18.5 us (4%)
  local copies, waits for them, and re-layouts  18.4 us (4%)
  other arithmetic  14.8 us (3%)
  between operations  14.6 us (3%)
    psum x1, blocking collectives, shards(): lax.psum(select_rows(low_terms, group_members).astype(jnp.bfloat16), 'mlp')  72.8 us
    all_gather x1, waiting for transfers between devices, shards(): whole = lax.all_gather(hidden_input, 'mlp', axis=1, tiled=True)  63.1 us
    all_gather x1, waiting for transfers between devices, shards(): kv_part = lax.all_gather(own_wkv, 'req', axis=0, tiled=True)  61.2 us
    all_gather x1, waiting for transfers between devices, shards(): lax.all_gather(output_weight, 'req', axis=2, tiled=True)  53.5 us
    all_gather x1, blocking collectives, shards(): lax.all_gather(request_key_value_up, 'req', axis=0, tiled=True)  36.1 us
    all_gather x1, blocking collectives, shards(): lax.all_gather(adapter_up_query, 'req', axis=0, tiled=True)  30.2 us
    all_gather x1, blocking collectives, shards(): lax.all_gather(adapter_up_output, 'req', axis=0, tiled=True)  30.1 us
    all_gather x1, blocking collectives, shards(): lax.all_gather(adapter_down_output, 'req', axis=0, tiled=True)  28.9 us
  transfers between devices with their start and end apart: 6, of which 4 were waited for; matrix products, arithmetic and copies ran while one was open for 9% of the time, Pallas kernels for 0%

profile of v1, /device:TPU:32, one launch (start us, length us, event | category | flops | bytes accessed | tf_op | source)
XLA Modules:
  0.0 470.5 jit_solution(2442774140966640459)
XLA Ops:
  7.3 0.7 all-gather.11.cloned.1.call-update
  8.0 0.2 copy-done
  8.2 0.7 constant_dynamic-slice_fusion.2
  9.0 0.7 all-gather.7.cloned.1.call-update
  9.7 0.5 all-gather.13.cloned.1.call-update
  10.3 0.5 all-gather.15.cloned.1.call-update
  10.9 0.7 fusion.90
  11.6 1.3 gather_fusion
  12.9 0.7 fusion.80
  13.5 0.7 compare_and_fusion
  14.2 0.8 reduce-window.4
  15.0 0.7 fusion.81
  15.8 0.6 fusion.76
  16.4 0.1 fusion.28
  16.5 0.7 constant_dynamic-slice_fusion.1
  17.3 36.1 %all_gather.36 = bf16[64,16,2,128]{3,1,2,0:T(8,128)(2,1)S(1)} all-gather(bf16[2,16,2,128]{3,1,2,0:T(8,128)(2,1)S(1)} %copy.66), channel_id=1, replica_groups=mesh['req'=32,'mlp'=16] {'req'}, dimensions={0}, use_global_device_ids=true | all-gather | bytes 540672 | tf_op jit(solution)/shard_map/all_gather | solution.py:106
  53.3 0.7 convert_element_type.104
  54.0 1.2 convert_element_type.113
  55.2 0.7 multiply_bitcast_fusion
  56.0 1.6 constant_dynamic-slice_fusion
  57.6 30.2 %all_gather.38 = bf16[64,16,256]{2,1,0:T(8,128)(2,1)S(1)} all-gather(bf16[2,16,256]{2,1,0:T(8,128)(2,1)S(1)} %copy-done.6), channel_id=1, replica_groups=mesh['req'=32,'mlp'=16] {'req'}, dimensions={0}, use_global_device_ids=true | all-gather | bytes 540672 | tf_op jit(solution)/shard_map/all_gather | solution.py:105
  87.8 0.5 convert_element_type.116
  88.4 0.1 convert_reduce_fusion
  88.5 0.2 convolution_compare_fusion
  88.7 0.7 copy.65
  89.4 0.6 gather_fusion.2
  90.0 0.7 copy_select_fusion
  90.7 1.2 gather_fusion.3
  91.8 0.8 multiply_cosine_fusion
  92.8 2.6 gather_fusion.1
  95.4 61.2 %all-gather.9.cloned.1.call-done = bf16[4096,2,128]{2,1,0:T(2,128)(2,1)} async-done(((bf16[128,2,128]{2,1,0:T(2,128)(2,1)}), bf16[4096,2,128]{2,1,0:T(2,128)(2,1)}) %all-gather.9.cloned.1.call-update) | async-done | bytes 2097168 | tf_op jit(solution)/shard_map/all_gather | solution.py:124
  156.6 4.7 %copy.61 = bf16[4096,2,128]{0,2,1:T(8,128)(2,1)S(1)} copy(bf16[4096,2,128]{2,1,0:T(2,128)(2,1)} %all-gather.9.cloned.1.call-done) | data formatting | bytes 4194304 | tf_op jit(solution)/shard_map/reshape | solution.py:128
  161.3 63.1 %all-gather.7.cloned.1.call-done = bf16[384,4096]{1,0:T(8,128)(2,1)} async-done(((bf16[384,256]{1,0:T(8,128)(2,1)}), bf16[384,4096]{1,0:T(8,128)(2,1)}) %all-gather.7.cloned.1.call-update) | async-done | bytes 3145744 | tf_op jit(solution)/shard_map/all_gather | solution.py:83
  224.4 2.7 fusion
  227.2 0.1 copy-done.1
  227.3 1.1 fusion.2
  228.4 1.6 copy-done.2
  230.0 0.9 fusion.26
  230.9 72.8 %psum.7 = bf16[384,48]{0,1:T(8,128)(2,1)S(1)} all-reduce(bf16[384,48]{0,1:T(8,128)(2,1)} %fusion.26), channel_id=1, replica_groups=mesh['req'=32,'mlp'=16] {'mlp'}, use_global_device_ids=true, to_apply=%region_4.5 | all-reduce | flops 18432 | bytes 73728 | tf_op jit(solution)/shard_map/psum | solution.py:122
  303.7 0.9 convolution_bitcast_fusion.2
  304.7 0.9 convolution_bitcast_fusion.3
  305.6 3.2 fusion.17
  309.0 0.4 fusion.46
  309.5 0.1 copy.53
  309.6 3.8 fusion.92
  313.5 0.4 multiply_reduce_fusion
  313.8 0.1 copy.54
  314.0 0.1 copy.52
  314.1 0.2 multiply_multiply_fusion
  314.3 0.2 subtract_convert_fusion
  314.5 0.9 fusion.5
  315.5 0.9 fusion.23
  316.4 53.5 %all-gather.15.cloned.1.call-done = bf16[256,16,256]{0,2,1:T(8,128)(2,1)} async-done(((bf16[256,16,8]{0,2,1:T(8,128)(2,1)}), bf16[256,16,256]{0,2,1:T(8,128)(2,1)}) %all-gather.15.cloned.1.call-update) | async-done | bytes 2097168 | tf_op jit(solution)/shard_map/all_gather | solution.py:205
  369.9 4.3 convolution_convert_fusion
  374.2 0.7 copy-done.7
  374.9 28.9 %all_gather.40 = bf16[64,16,256]{2,1,0:T(8,128)(2,1)S(1)} all-gather(bf16[2,16,256]{2,1,0:T(8,128)(2,1)S(1)} %copy-done.7), channel_id=1, replica_groups=mesh['req'=32,'mlp'=16] {'req'}, dimensions={0}, use_global_device_ids=true | all-gather | bytes 540672 | tf_op jit(solution)/shard_map/all_gather | solution.py:104
  403.8 0.5 gather_fusion.4
  404.3 30.1 %all_gather.43 = bf16[64,16,256]{2,1,0:T(8,128)(2,1)S(1)} all-gather(bf16[2,16,256]{2,1,0:T(8,128)(2,1)S(1)} %copy-done.8), channel_id=1, replica_groups=mesh['req'=32,'mlp'=16] {'req'}, dimensions={0}, use_global_device_ids=true | all-gather | bytes 540672 | tf_op jit(solution)/shard_map/all_gather | solution.py:107
  434.4 0.5 gather_fusion.5
  435.0 0.2 fusion.27
  435.2 24.6 %all-gather = f32[6144,16]{0,1:T(8,128)S(1)} all-gather(f32[384,16]{0,1:T(8,128)S(1)} %fusion.27), channel_id=2, replica_groups=mesh['req'=32,'mlp'=16] {'mlp'}, dimensions={0}, use_global_device_ids=true | all-gather | bytes 417792 | tf_op jit(solution)/shard_map/all_gather | solution.py:198
  459.9 0.7 fusion.50
  460.7 1.1 reduce-scatter.2.cloned.1.call-done
  461.8 1.9 fusion.16
  (64 shorter events, 1.2 us)
Async XLA Ops:
  7.2 1.1 copy-start
  7.2 81.2 %copy-start.17 = (s32[1,4]{1,0:T(1,128)S(1)}, s32[1,4]{1,0:T(1,128)}, u32[]{:S(2)}) copy-start(s32[1,4]{1,0:T(1,128)} %param.34) | copy-start | bytes 52
  7.2 50.4 %copy-start.6 = (bf16[2,16,256]{2,1,0:T(8,128)(2,1)S(1)}, bf16[2,16,256]{2,1,0:T(8,128)(2,1)}, u32[]{:S(2)}) copy-start(bf16[2,16,256]{2,1,0:T(8,128)(2,1)} %param.29) | copy-start | bytes 49156
  7.2 80.6 %copy-start.16 = (bf16[128]{0:T(256)(128)(2,1)S(1)}, bf16[128]{0:T(256)(128)(2,1)}, u32[]{:S(2)}) copy-start(bf16[128]{0:T(256)(128)(2,1)} %param.22) | copy-start | bytes 772
  7.2 81.2 %copy-start.13 = (s32[1,4,8]{2,1,0:T(4,128)S(1)}, s32[1,4,8]{2,1,0:T(4,128)}, u32[]{:S(2)}) copy-start(s32[1,4,8]{2,1,0:T(4,128)} %param.35) | copy-start | bytes 388
  7.2 85.5 %all-gather.11.cloned.1.call-start = ((), (), s32[]{:S(2)}) async-start(), calls=%async_computation.3 | async-start | bytes 1622016 | tf_op jit(solution)/shard_map/all_gather | solution.py:103
  8.0 148.6 %all-gather.9.cloned.1.call-start = ((), (), s32[]{:S(2)}) async-start(), calls=%async_computation.2 | async-start | bytes 2162688 | tf_op jit(solution)/shard_map/all_gather | solution.py:124
  8.9 215.5 %all-gather.7.cloned.1.call-start = ((), (), s32[]{:S(2)}) async-start(), calls=%async_computation.1 | async-start | bytes 3342336 | tf_op jit(solution)/shard_map/all_gather | solution.py:83
  9.7 299.9 %all-gather.13.cloned.1.call-start = ((), (), s32[]{:S(2)}) async-start(), calls=%async_computation.4 | async-start | bytes 2162688 | tf_op jit(solution)/shard_map/all_gather | solution.py:123
  10.3 359.6 %all-gather.15.cloned.1.call-start = ((), (), s32[]{:S(2)}) async-start(), calls=%async_computation.5 | async-start | bytes 2162688 | tf_op jit(solution)/shard_map/all_gather | solution.py:205
  10.8 450.9 %reduce-scatter.2.cloned.1.call-start = ((), (), s32[]{:S(2)}) async-start(), calls=%async_computation.6 | async-start | bytes 3342336 | tf_op jit(solution)/shard_map/reduce_scatter | solution.py:208
  14.2 147.1 %copy-start.11 = (f32[64]{0:T(128)}, f32[64]{0:T(128)S(1)}, u32[]{:S(2)}) copy-start(f32[64]{0:T(128)S(1)} %multiply_exponential_fusion) | copy-start | bytes 772
  224.4 2.8 copy-start.1
  227.3 2.8 copy-start.5
  227.3 2.8 copy-start.9
  228.4 1.7 copy-start.2
  305.6 3.3 copy-start.14
  305.6 3.4 copy-start.12
  309.6 3.9 copy-start.4
  309.6 4.5 copy-start.15
  314.3 1.2 copy-start.3
  374.1 0.7 copy-start.7
  374.1 30.2 %copy-start.8 = (bf16[2,16,256]{2,1,0:T(8,128)(2,1)S(1)}, bf16[2,16,256]{2,1,0:T(8,128)(2,1)}, u32[]{:S(2)}) copy-start(bf16[2,16,256]{2,1,0:T(8,128)(2,1)} %param.31) | copy-start | bytes 49156
  374.1 60.9 %copy-start.10 = (f32[384,4]{0,1:T(4,128)S(1)}, f32[384,4]{0,1:T(4,128)}, u32[]{:S(2)}) copy-start(f32[384,4]{0,1:T(4,128)} %get-tuple-element.17) | copy-start | bytes 18436
Sparse Core Ops, SparseCore 0:
  10.2 75.3 all-gather.10
  87.7 68.8 all-gather.8
  159.6 64.8 all-gather.6
  226.4 71.1 all-gather.12
  299.5 70.3 all-gather.14
  374.3 87.4 reduce-scatter.1
